TPU v7x, 128 devices: a whole 4x4x4 slice. The times are simulated.
128 devices in a mesh: dp: 16 (over z, y), tensor: 8 (over x, core).
Axes of the slice: x: 4, y: 4, z: 4, core: 2. Of those that a mesh axis runs over, the one named last changes fastest.
Arguments:
- dense: bfloat16 [3072, 2048], P('dp'), may hold values from -8 to 8
- bottom_weight: bfloat16 [2048, 16384], P(None, 'tensor'), may hold values from -0.125 to 0.125
- bottom_bias: float32 [16384], P('tensor'), may hold values from -3 to 3
- cross_blocks: bfloat16 [80, 512, 512], P('tensor', 'dp'), may hold values from -0.25 to 0.25
- cross_bias: float32 [16384], P('tensor'), may hold values from -3 to 3
- cotangent: bfloat16 [3072, 16384], P('dp', 'tensor'), may hold values from -6 to 6
- in_blocks: int32 [8, 10], replicated, may hold values from 0 to 31, as said below
- out_blocks: int32 [8, 10], replicated, may hold values from 0 to 31, as said below
- live_slots: int32 [8], replicated, may hold values from 2 to 10, as said below
Outputs:
- cross_out: bfloat16 [3072, 16384], P('dp', 'tensor')
- grad_bottom: float32 [2048, 16384], P('dp', 'tensor')
- grad_bias_bottom: float32 [16384], P('tensor')
- grad_blocks: float32 [80, 512, 512], P('tensor', 'dp')
- grad_bias: float32 [16384], P('tensor')
Inputs may be any that keep to these rules, and one draw needn't show every extreme that they name: `in_blocks`: among the live slots of one tensor device, at most 2 have input blocks held by any one tensor device (blocks s * 16384 / (512 * 8) onward for device s), and this most is reached in every draw. `out_blocks`: among the live slots of one tensor device, at most 2 have output blocks held by any one tensor device, and this most is reached in every draw. `live_slots`: some tensor device has all 10 slots live.
All inputs are finite; a program needn't handle non-finite values.
Results may differ from a plain program's by a relative error of at most 0.014.
Values may be sent and summed in bfloat16 or wider, within the bound.
A program may use at most 128 MiB of HBM per device.

v0:
```python
import jax
import jax.numpy as jnp
from jax import lax
from jax.sharding import PartitionSpec as P

BLK = 512
SLOTS = 10


def slot_ranks(owner, alive):
    order = jnp.arange(owner.shape[1])
    earlier = order[None, :] < order[:, None]
    same = (owner[:, :, None] == owner[:, None, :]) & alive[:, None, :] & earlier[None, :, :]
    return jnp.sum(same.astype(jnp.int32), axis=2)


def post_table(owner_mine, rank_mine, alive_mine, groups, capacity):
    slot_count = owner_mine.shape[0]
    match = (
        (owner_mine[None, None, :] == jnp.arange(groups)[:, None, None])
        & (rank_mine[None, None, :] == jnp.arange(capacity)[None, :, None])
        & alive_mine[None, None, :]
    )
    chosen = jnp.sum(match.astype(jnp.int32) * jnp.arange(slot_count)[None, None, :], axis=2)
    filled = jnp.any(match, axis=2)
    return (chosen, filled)


def pack_parts(parts, chosen, filled):
    picked = jnp.take(parts, chosen.reshape(-1), axis=0) * filled.reshape(-1)[:, None, None].astype(
        parts.dtype
    )
    return picked.reshape(chosen.shape[0], chosen.shape[1] * parts.shape[1], parts.shape[2])


def collect_parts(received, owner, local, rank, alive, target, capacity, per_device):
    groups, span_rows, block_width = received.shape
    row_count = span_rows // capacity
    match = ((owner == target) & alive)[:, :, None] & (
        rank[:, :, None] == jnp.arange(capacity)[None, None, :]
    )
    matches = match[:, :, :, None] & (
        local[:, :, None, None] == jnp.arange(per_device)[None, None, None, :]
    )
    onehot = (
        jnp.sum(matches.astype(jnp.int32), axis=1)
        .reshape(groups * capacity, per_device)
        .astype(jnp.bfloat16)
    )
    flattened = received.reshape(groups * capacity, row_count, block_width)
    summed = jnp.einsum("irb,il->rlb", flattened, onehot, preferred_element_type=jnp.float32)
    return summed.reshape(row_count, per_device * block_width)


def ring_gather(x, axis, n):
    half = x.shape[0] // 2
    right = [(i, (i + 1) % n) for i in range(n)]
    left = [(i, (i - 1) % n) for i in range(n)]
    cur_a, cur_b = (x[:half], x[half:])
    outs_a, outs_b = ([cur_a], [cur_b])
    for _ in range(1, n):
        cur_a = lax.ppermute(cur_a, axis, right)
        cur_b = lax.ppermute(cur_b, axis, left)
        outs_a.append(cur_a)
        outs_b.append(cur_b)
    return (jnp.stack(outs_a), jnp.stack(outs_b))


def take_blocks(stack_a, stack_b, owner, local, me, n):
    steps, half, width = stack_a.shape
    blocks_a = stack_a.reshape(steps, half, width // BLK, BLK)
    blocks_b = stack_b.reshape(steps, half, width // BLK, BLK)
    step_a = (me - owner) % n
    step_b = (owner - me) % n
    top = blocks_a[step_a, :, local, :]
    bottom = blocks_b[step_b, :, local, :]
    return jnp.concatenate([top, bottom], axis=1)


def on_device(
    dense,
    bottom_weight,
    bottom_bias,
    cross_blocks,
    cross_bias,
    cotangent,
    in_blocks,
    out_blocks,
    live_slots,
):
    groups = lax.axis_size("tensor")
    mine = lax.axis_index("tensor")
    row_count = dense.shape[0]
    local_width = bottom_weight.shape[1]
    per_device = local_width // BLK
    capacity = -(-SLOTS // groups)
    preact = jnp.dot(dense, bottom_weight, preferred_element_type=jnp.float32) + bottom_bias
    start = jax.nn.silu(preact).astype(jnp.bfloat16)
    start_wide = start.astype(jnp.float32)
    cot_wide = cotangent.astype(jnp.float32)
    grad_mixed = cot_wide * start_wide
    grad_mixed_low = grad_mixed.astype(jnp.bfloat16)
    alive = jnp.arange(SLOTS)[None, :] < live_slots[:, None]
    alive_mine = alive[mine]
    switch = alive_mine.astype(jnp.bfloat16)[:, None, None]
    in_owner = in_blocks // per_device
    in_local = in_blocks % per_device
    out_owner = out_blocks // per_device
    out_local = out_blocks % per_device
    in_rank = slot_ranks(in_owner, alive)
    out_rank = slot_ranks(out_owner, alive)
    combo = jnp.concatenate([start, grad_mixed_low], axis=1)
    stack_a, stack_b = ring_gather(combo, "tensor", groups)
    fetched = take_blocks(stack_a, stack_b, in_owner[mine], in_local[mine], mine, groups)
    taken = fetched
    product = jnp.einsum(
        "kri,kij->krj",
        taken,
        lax.all_gather(cross_blocks, "dp", axis=1, tiled=True),
        preferred_element_type=jnp.float32,
    )
    parts = product.astype(jnp.bfloat16) * switch
    chosen_out, filled_out = post_table(
        out_owner[mine], out_rank[mine], alive_mine, groups, capacity
    )
    arrived_parts = lax.all_to_all(
        pack_parts(parts, chosen_out, filled_out), "tensor", split_axis=0, concat_axis=0, tiled=True
    )
    mixed = (
        collect_parts(
            arrived_parts, out_owner, out_local, out_rank, alive, mine, capacity, per_device
        )
        + cross_bias
    )
    cross_out = (start_wide * mixed + start_wide).astype(jnp.bfloat16)
    upstream = take_blocks(
        stack_a, stack_b, out_owner[mine], out_local[mine] + per_device, mine, groups
    )
    upstream = upstream * switch
    backward = jnp.einsum(
        "krj,kij->kri",
        upstream,
        lax.all_gather(cross_blocks, "dp", axis=1, tiled=True),
        preferred_element_type=jnp.float32,
    )
    back_parts = backward.astype(jnp.bfloat16)
    chosen_in, filled_in = post_table(in_owner[mine], in_rank[mine], alive_mine, groups, capacity)
    arrived_back = lax.all_to_all(
        pack_parts(back_parts, chosen_in, filled_in),
        "tensor",
        split_axis=0,
        concat_axis=0,
        tiled=True,
    )
    grad_start = collect_parts(
        arrived_back, in_owner, in_local, in_rank, alive, mine, capacity, per_device
    )
    block_terms = jnp.einsum("kri,krj->kij", fetched, upstream, preferred_element_type=jnp.float32)
    grad_blocks = lax.psum_scatter(
        block_terms.astype(jnp.bfloat16), "dp", scatter_dimension=1, tiled=True
    ).astype(jnp.float32)
    grad_start = grad_start + cot_wide * mixed + cot_wide
    sigma = jax.nn.sigmoid(preact)
    grad_pre = grad_start * sigma * (1.0 + preact * (1.0 - sigma))
    grad_pre_low = grad_pre.astype(jnp.bfloat16)
    taken = dense
    grad_bottom = lax.psum_scatter(
        lax.dot_general(
            taken, grad_pre_low, (((0,), (0,)), ((), ())), preferred_element_type=jnp.float32
        ).astype(jnp.bfloat16),
        "dp",
        scatter_dimension=0,
        tiled=True,
    ).astype(jnp.float32)
    bias_sums = lax.psum((jnp.sum(grad_pre, axis=0), jnp.sum(grad_mixed, axis=0)), "dp")
    return (cross_out, grad_bottom, bias_sums[0], grad_blocks, bias_sums[1])


def solution(mesh):
    return jax.shard_map(
        on_device,
        mesh=mesh,
        in_specs=(
            P("dp", None),
            P(None, "tensor"),
            P("tensor"),
            P("tensor", "dp", None),
            P("tensor"),
            P("dp", "tensor"),
            P(),
            P(),
            P(),
        ),
        out_specs=(
            P("dp", "tensor"),
            P("dp", "tensor"),
            P("tensor"),
            P("tensor", "dp", None),
            P("tensor"),
        ),
        check_vma=False,
    )
```

profile of v0, /device:TPU:0, one launch (start us, length us, event | category | flops | bytes accessed | tf_op | source)
XLA Modules:
  0.0 354.9 jit_solution(3943194718781024249)
XLA Ops:
  7.2 0.7 all-gather.2.cloned.1.call-update
  8.3 7.5 %fusion.8 = (f32[2048]{0:T(1024)}, bf16[192,2048]{1,0:T(8,128)(2,1)S(1)}, f32[192,2048]{1,0:T(8,128)}) fusion(bf16[192,2048]{1,0:T(8,128)(2,1)} %param.16, f32[2048]{0:T(1024)} %param.13, bf16[192,2048]{1,0:T(8,128)(2,1)S(1)} %copy-done, bf16[2048,2048]{1,0:T(8,128)(2,1)} %param.12), kind=kOutput, calls=%fused_computation.30 | convolution fusion | flops 1614542848 | bytes 12337152 | tf_op jit(solution)/shard_map/dot_general | solution.py:97
  16.3 2.9 collective-permute-start.7
  19.3 9.8 %collective-permute-done = bf16[96,4096]{1,0:T(8,128)(2,1)} collective-permute-done((bf16[96,4096]{1,0:T(8,128)(2,1)S(1)}, bf16[96,4096]{1,0:T(8,128)(2,1)}, u32[]{:S(2)}, u32[]{:S(2)}) %collective-permute-start) | collective-permute-done | bytes 786464 | tf_op jit(solution)/shard_map/ppermute | solution.py:62
  29.1 3.0 collective-permute-start.8
  32.1 0.6 compare_and_fusion.1
  32.7 9.3 %collective-permute-done.1 = bf16[96,4096]{1,0:T(8,128)(2,1)} collective-permute-done((bf16[96,4096]{1,0:T(8,128)(2,1)}, bf16[96,4096]{1,0:T(8,128)(2,1)}, u32[]{:S(2)}, u32[]{:S(2)}) %collective-permute-start.1) | collective-permute-done | bytes 786464 | tf_op jit(solution)/shard_map/ppermute | solution.py:62
  42.0 3.0 collective-permute-start.9
  45.0 1.4 copy.127
  46.4 1.4 copy.135
  48.9 1.4 copy.128
  50.3 1.4 copy.136
  51.8 3.2 collective-permute-done.2
  55.0 3.2 collective-permute-start.10
  58.7 1.4 copy.129
  60.1 1.4 copy.137
  61.8 6.0 %collective-permute-done.3 = bf16[96,4096]{1,0:T(8,128)(2,1)S(1)} collective-permute-done((bf16[96,4096]{1,0:T(8,128)(2,1)}, bf16[96,4096]{1,0:T(8,128)(2,1)S(1)}, u32[]{:S(2)}, u32[]{:S(2)}) %collective-permute-start.3) | collective-permute-done | bytes 786464 | tf_op jit(solution)/shard_map/ppermute | solution.py:62
  68.0 3.2 collective-permute-start.11
  71.5 1.4 copy.130
  72.9 1.4 copy.138
  75.4 5.0 %collective-permute-done.4 = bf16[96,4096]{1,0:T(8,128)(2,1)S(1)} collective-permute-done((bf16[96,4096]{1,0:T(8,128)(2,1)S(1)}, bf16[96,4096]{1,0:T(8,128)(2,1)S(1)}, u32[]{:S(2)}, u32[]{:S(2)}) %collective-permute-start.4) | collective-permute-done | bytes 786464 | tf_op jit(solution)/shard_map/ppermute | solution.py:62
  80.8 3.1 collective-permute-start.12
  85.2 7.9 %collective-permute-done.5 = bf16[96,4096]{1,0:T(8,128)(2,1)S(1)} collective-permute-done((bf16[96,4096]{1,0:T(8,128)(2,1)S(1)}, bf16[96,4096]{1,0:T(8,128)(2,1)S(1)}, u32[]{:S(2)}, u32[]{:S(2)}) %collective-permute-start.5) | collective-permute-done | bytes 786464 | tf_op jit(solution)/shard_map/ppermute | solution.py:62
  93.4 3.1 collective-permute-start.13
  97.8 7.9 %collective-permute-done.6 = bf16[96,4096]{1,0:T(8,128)(2,1)S(1)} collective-permute-done((bf16[96,4096]{1,0:T(8,128)(2,1)S(1)}, bf16[96,4096]{1,0:T(8,128)(2,1)S(1)}, u32[]{:S(2)}, u32[]{:S(2)}) %collective-permute-start.6) | collective-permute-done | bytes 786464 | tf_op jit(solution)/shard_map/ppermute | solution.py:62
  106.6 2.6 copy-done.8
  109.2 3.4 gather_fusion
  112.6 4.4 %gather_fusion.2 = bf16[10,96,512]{2,1,0:T(8,128)(2,1)} fusion(bf16[8,96,8,512]{3,1,2,0:T(8,128)(2,1)} %copy-done.8, s32[10]{0:T(128)S(1)} %get-tuple-element.52), kind=kCustom, calls=%fused_computation.4 | custom fusion | bytes 1966160 | tf_op jit(solution)/shard_map/gather | solution.py:75
  117.0 1.1 copy_dynamic-update-slice_fusion
  118.1 3.4 gather_fusion.1
  121.6 4.4 %gather_fusion.3 = bf16[10,96,512]{2,1,0:T(8,128)(2,1)} fusion(bf16[8,96,8,512]{3,1,2,0:T(8,128)(2,1)} %copy_dynamic-update-slice_fusion, s32[10]{0:T(128)S(1)} %get-tuple-element.53), kind=kCustom, calls=%fused_computation.5 | custom fusion | bytes 1966160 | tf_op jit(solution)/shard_map/gather | solution.py:76
  126.3 1.3 copy-done.1
  128.1 4.1 %convolution_convert_fusion = bf16[10,512,512]{2,1,0:T(8,128)(2,1)} fusion(bf16[10,192,512]{2,1,0:T(8,128)(2,1)S(1)} %constant_dynamic-update-slice_fusion, bf16[10,96,512]{2,1,0:T(8,128)(2,1)S(1)} %copy-done.10, bf16[10,96,512]{2,1,0:T(8,128)(2,1)S(1)} %copy-done.9, bf16[10]{0:T(256)(128)(2,1)S(1)} %copy-done.19), kind=kOutput, calls=%fused_computation.13 | convolution fusion | flops 1015152640 | bytes 9175060 | tf_op jit(solution)/shard_map/kri,krj->kij/dot_general | solution.py:158
  132.8 1.2 convert_reduce_fusion
  134.2 0.7 fusion.47
  134.9 0.7 select_reduce_fusion
  135.8 0.7 fusion.16
  136.6 0.7 reshape.558
  137.3 0.6 pad_clamp_fusion.1
  138.4 4.3 %convert_multiply_fusion.2 = bf16[10,192,512]{2,1,0:T(8,128)(2,1)S(1)} fusion(bf16[10,192,512]{2,1,0:T(8,128)(2,1)} %copy-done.1, bf16[10,512,512]{2,1,0:T(8,128)(2,1)} %all-gather.2.cloned.1.call-done, bf16[10]{0:T(256)(128)(2,1)} %get-tuple-element.45), kind=kOutput, calls=%fused_computation.20 | convolution fusion | flops 1008599040 | bytes 9175060 | tf_op jit(solution)/shard_map/kri,kij->krj/dot_general | solution.py:116
  142.7 2.5 gather_fusion.4
  145.3 3.9 %select_multiply_fusion.1 = bf16[16,192,512]{2,1,0:T(8,128)(2,1)} fusion(bf16[16,192,512]{2,1,0:T(8,128)(2,1)} %gather_fusion.4, pred[16]{0:T(512)(128)(4,1)} %compare_and_fusion.3, bf16[16]{0:T(256)(128)(2,1)} %reshape.558), kind=kLoop, calls=%fused_computation.12 | loop fusion | flops 3145728 | bytes 6291504 | tf_op jit(solution)/shard_map/mul | solution.py:30
  149.2 4.6 %all-to-all-start = ((bf16[8,384,512]{2,1,0:T(8,128)(2,1)}), bf16[8,384,512]{2,1,0:T(8,128)(2,1)}, u32[]{:S(2)}, u32[]{:S(2)}) async-start(bf16[8,384,512]{2,1,0:T(8,128)(2,1)} %bitcast.135), calls=%async_computation | async-start | bytes 6291456 | tf_op jit(solution)/shard_map/all_to_all | solution.py:126
  154.1 0.6 reshape.559
  154.7 0.6 pad_clamp_fusion
  155.8 5.3 %convolution_convert_fusion.1 = bf16[10,192,512]{2,1,0:T(8,128)(2,1)S(1)} fusion(bf16[10,512,512]{2,1,0:T(8,128)(2,1)} %all-gather.2.cloned.1.call-done, bf16[10,96,512]{2,1,0:T(8,128)(2,1)} %gather_fusion.3, bf16[10,96,512]{2,1,0:T(8,128)(2,1)} %gather_fusion.2, bf16[10]{0:T(256)(128)(2,1)} %get-tuple-element.45), kind=kOutput, calls=%fused_computation.21 | convolution fusion | flops 1013514240 | bytes 9175060 | tf_op jit(solution)/shard_map/krj,kij->kri/dot_general | solution.py:140
  161.1 2.6 gather_fusion.5
  163.7 4.0 %select_multiply_fusion = bf16[16,192,512]{2,1,0:T(8,128)(2,1)} fusion(bf16[16,192,512]{2,1,0:T(8,128)(2,1)} %gather_fusion.5, pred[16]{0:T(512)(128)(4,1)} %compare_and_fusion.2, bf16[16]{0:T(256)(128)(2,1)} %reshape.559), kind=kLoop, calls=%fused_computation.11 | loop fusion | flops 3145728 | bytes 6291504 | tf_op jit(solution)/shard_map/mul | solution.py:30
  167.7 24.5 %all-to-all-done = bf16[8,384,512]{2,1,0:T(8,128)(2,1)} async-done(((bf16[8,384,512]{2,1,0:T(8,128)(2,1)}), bf16[8,384,512]{2,1,0:T(8,128)(2,1)}, u32[]{:S(2)}, u32[]{:S(2)}) %all-to-all-start) | async-done | bytes 3145760 | tf_op jit(solution)/shard_map/all_to_all | solution.py:126
  192.3 4.6 %all-to-all-start.1 = ((bf16[8,384,512]{2,1,0:T(8,128)(2,1)}), bf16[8,384,512]{2,1,0:T(8,128)(2,1)}, u32[]{:S(2)}, u32[]{:S(2)}) async-start(bf16[8,384,512]{2,1,0:T(8,128)(2,1)} %bitcast.134), calls=%async_computation.1 | async-start | bytes 6291456 | tf_op jit(solution)/shard_map/all_to_all | solution.py:148
  197.8 3.8 %fusion.2 = f32[4,192,512]{2,0,1:T(4,128)S(1)} fusion(bf16[16,4,1]{1,0,2:T(8,128)(2,1)S(1)} %bitcast.166, bf16[16,192,512]{2,1,0:T(8,128)(2,1)} %bitcast.10), kind=kOutput, calls=%fused_computation.9 | convolution fusion | flops 12582912 | bytes 4718720 | tf_op jit(solution)/shard_map/irb,il->rlb/dot_general | solution.py:51
  201.6 0.6 copy.143
  202.2 33.1 %all-to-all-done.1 = bf16[8,384,512]{2,1,0:T(8,128)(2,1)} async-done(((bf16[8,384,512]{2,1,0:T(8,128)(2,1)}), bf16[8,384,512]{2,1,0:T(8,128)(2,1)}, u32[]{:S(2)}, u32[]{:S(2)}) %all-to-all-start.1) | async-done | bytes 3145760 | tf_op jit(solution)/shard_map/all_to_all | solution.py:148
  235.3 4.0 %fusion = f32[4,192,512]{2,0,1:T(4,128)S(1)} fusion(bf16[16,4,1]{1,0,2:T(8,128)(2,1)S(1)} %bitcast.167, bf16[16,192,512]{2,1,0:T(8,128)(2,1)} %bitcast.22), kind=kOutput, calls=%fused_computation.7 | convolution fusion | flops 12582912 | bytes 4718720 | tf_op jit(solution)/shard_map/irb,il->rlb/dot_general | solution.py:51
  239.3 0.6 copy.144
  239.9 1.9 fusion.49
  241.8 5.6 %convert_bitcast_fusion = bf16[2048,2048]{0,1:T(8,128)(2,1)} fusion(bf16[192,2048]{1,0:T(8,128)(2,1)S(1)} %copy-done, bf16[192,2048]{1,0:T(8,128)(2,1)S(1)} %get-tuple-element.42), kind=kOutput, calls=%fused_computation.6 | convolution fusion | flops 1614807040 | bytes 9961472 | tf_op jit(solution)/shard_map/dot_general | solution.py:168
  247.4 12.4 %copy.125 = bf16[2048,2048]{1,0:T(8,128)(2,1)} copy(bf16[2048,2048]{0,1:T(8,128)(2,1)} %convert_bitcast_fusion) | data formatting | bytes 16777216
  259.8 0.7 copy-done.20
  260.5 76.5 %all-reduce = (f32[2048]{0:T(1024)}, f32[2048]{0:T(1024)}) all-reduce(f32[2048]{0:T(1024)S(1)} %get-tuple-element.41, f32[2048]{0:T(1024)S(1)} %copy-done.20), channel_id=1, replica_groups=mesh['dp'=16,'tensor'=8] {'dp'}, use_global_device_ids=true, to_apply=%region_10.12 | all-reduce | flops 4096 | bytes 32768 | tf_op jit(solution)/shard_map/psum | solution.py:175
  337.0 1.9 convert_element_type.131
  338.9 7.0 %reduce-scatter.7.cloned.1.call-done = bf16[128,2048]{1,0:T(8,128)(2,1)} async-done(((bf16[2048,2048]{1,0:T(8,128)(2,1)}), bf16[128,2048]{1,0:T(8,128)(2,1)}) %reduce-scatter.7.cloned.1.call-update) | async-done | bytes 524304
  345.9 1.3 copy.126
  347.2 1.2 copy.120
  (140 shorter events, 12.5 us)
Async XLA Ops:
  7.2 1.1 copy-start
  7.2 131.2 %all-gather.2.cloned.1.call-start = ((), (), s32[]{:S(2)}) async-start(), calls=%async_computation.4 | async-start | bytes 5570560 | tf_op jit(solution)/shard_map/all_gather | solution.py:119
  7.9 7.9 %copy-start.4 = (bf16[192,2048]{1,0:T(8,128)(2,1)S(1)}, bf16[192,2048]{1,0:T(8,128)(2,1)}, u32[]{:S(2)}) copy-start(bf16[192,2048]{1,0:T(8,128)(2,1)} %param.16) | copy-start | bytes 2359300
  7.9 329.0 %reduce-scatter.5.cloned.1.call-start = ((), (), s32[]{:S(2)}) async-start(), calls=%async_computation.5 | async-start | bytes 5570560 | tf_op jit(solution)/shard_map/reduce_scatter | solution.py:159
  15.9 16.2 %copy-start.17 = (s32[8,10]{1,0:T(8,128)S(1)}, s32[8,10]{1,0:T(8,128)}, u32[]{:S(2)}) copy-start(s32[8,10]{1,0:T(8,128)} %param.17) | copy-start | bytes 964
  15.9 16.2 %copy-start.18 = (s32[8,10]{1,0:T(8,128)S(1)}, s32[8,10]{1,0:T(8,128)}, u32[]{:S(2)}) copy-start(s32[8,10]{1,0:T(8,128)} %param.18) | copy-start | bytes 964
  15.9 16.2 %copy-start.28 = (s32[8]{0:T(128)S(1)}, s32[8]{0:T(128)}, u32[]{:S(2)}) copy-start(s32[8]{0:T(128)} %param.19) | copy-start | bytes 100
  16.3 28.7 %copy-start.3 = (bf16[96,4096]{1,0:T(8,128)(2,1)}, bf16[96,4096]{1,0:T(8,128)(2,1)S(1)}, u32[]{:S(2)}) copy-start(bf16[96,4096]{1,0:T(8,128)(2,1)S(1)} %get-tuple-element.51) | copy-start | bytes 2359300
  16.3 30.1 %copy-start.2 = (bf16[96,4096]{1,0:T(8,128)(2,1)}, bf16[96,4096]{1,0:T(8,128)(2,1)S(1)}, u32[]{:S(2)}) copy-start(bf16[96,4096]{1,0:T(8,128)(2,1)S(1)} %get-tuple-element.50) | copy-start | bytes 2359300
  16.3 12.7 %collective-permute-start = (bf16[96,4096]{1,0:T(8,128)(2,1)S(1)}, bf16[96,4096]{1,0:T(8,128)(2,1)}, u32[]{:S(2)}, u32[]{:S(2)}) collective-permute-start(bf16[96,4096]{1,0:T(8,128)(2,1)S(1)} %get-tuple-element.51), channel_id=1, source_target_pairs={{0,1},{1,2},{2,3},{3,4},{4,5},{5,6},{6,7},{7,0},{8,9},{9,10},{10,1... | collective-permute-start | bytes 2359304 | tf_op jit(solution)/shard_map/ppermute | solution.py:62
  16.3 12.7 %collective-permute-start.7 = (bf16[96,4096]{1,0:T(8,128)(2,1)S(1)}, bf16[96,4096]{1,0:T(8,128)(2,1)}, u32[]{:S(2)}, u32[]{:S(2)}) collective-permute-start(bf16[96,4096]{1,0:T(8,128)(2,1)S(1)} %get-tuple-element.50), channel_id=1, source_target_pairs={{0,7},{1,0},{2,1},{3,2},{4,3},{5,4},{6,5},{7,6},{8,15},{9,8},{10,9... | collective-permute-start | bytes 2359304 | tf_op jit(solution)/shard_map/ppermute | solution.py:63
  29.1 12.9 %collective-permute-start.1 = (bf16[96,4096]{1,0:T(8,128)(2,1)}, bf16[96,4096]{1,0:T(8,128)(2,1)}, u32[]{:S(2)}, u32[]{:S(2)}) collective-permute-start(bf16[96,4096]{1,0:T(8,128)(2,1)} %collective-permute-done), channel_id=1, source_target_pairs={{0,1},{1,2},{2,3},{3,4},{4,5},{5,6},{6,7},{7,0},{8,9},{9,10},{10,1... | collective-permute-start | bytes 2359304 | tf_op jit(solution)/shard_map/ppermute | solution.py:62
  29.1 12.9 %collective-permute-start.8 = (bf16[96,4096]{1,0:T(8,128)(2,1)}, bf16[96,4096]{1,0:T(8,128)(2,1)}, u32[]{:S(2)}, u32[]{:S(2)}) collective-permute-start(bf16[96,4096]{1,0:T(8,128)(2,1)} %collective-permute-done.7), channel_id=1, source_target_pairs={{0,7},{1,0},{2,1},{3,2},{4,3},{5,4},{6,5},{7,6},{8,15},{9,8},{10,9... | collective-permute-start | bytes 2359304 | tf_op jit(solution)/shard_map/ppermute | solution.py:63
  32.1 16.9 %copy-start.13 = (s32[8,10]{1,0:T(8,128)}, s32[8,10]{1,0:T(8,128)S(1)}, u32[]{:S(2)}) copy-start(s32[8,10]{1,0:T(8,128)S(1)} %add_select_fusion) | copy-start | bytes 964
  32.7 16.2 %copy-start.22 = (pred[8,10]{1,0:T(8,128)(4,1)}, pred[8,10]{1,0:T(8,128)(4,1)S(1)}, u32[]{:S(2)}) copy-start(pred[8,10]{1,0:T(8,128)(4,1)S(1)} %get-tuple-element.58) | copy-start | bytes 244
  32.7 99.4 %copy-start.12 = (s32[8,10]{1,0:T(8,128)}, s32[8,10]{1,0:T(8,128)S(1)}, u32[]{:S(2)}) copy-start(s32[8,10]{1,0:T(8,128)S(1)} %get-tuple-element.57) | copy-start | bytes 964
  32.7 99.5 %copy-start.11 = (s32[8,10]{1,0:T(8,128)}, s32[8,10]{1,0:T(8,128)S(1)}, u32[]{:S(2)}) copy-start(s32[8,10]{1,0:T(8,128)S(1)} %get-tuple-element.48) | copy-start | bytes 964
  42.0 12.9 %collective-permute-start.2 = (bf16[96,4096]{1,0:T(8,128)(2,1)}, bf16[96,4096]{1,0:T(8,128)(2,1)}, u32[]{:S(2)}, u32[]{:S(2)}) collective-permute-start(bf16[96,4096]{1,0:T(8,128)(2,1)} %collective-permute-done.1), channel_id=1, source_target_pairs={{0,1},{1,2},{2,3},{3,4},{4,5},{5,6},{6,7},{7,0},{8,9},{9,10},{10,1... | collective-permute-start | bytes 2359304 | tf_op jit(solution)/shard_map/ppermute | solution.py:62
  42.0 12.9 %collective-permute-start.9 = (bf16[96,4096]{1,0:T(8,128)(2,1)}, bf16[96,4096]{1,0:T(8,128)(2,1)}, u32[]{:S(2)}, u32[]{:S(2)}) collective-permute-start(bf16[96,4096]{1,0:T(8,128)(2,1)} %collective-permute-done.8), channel_id=1, source_target_pairs={{0,7},{1,0},{2,1},{3,2},{4,3},{5,4},{6,5},{7,6},{8,15},{9,8},{10,9... | collective-permute-start | bytes 2359304 | tf_op jit(solution)/shard_map/ppermute | solution.py:63
  45.0 4.0 %copy-start.15 = (s32[8,10]{1,0:T(8,128)}, s32[8,10]{1,0:T(8,128)S(1)}, u32[]{:S(2)}) copy-start(s32[8,10]{1,0:T(8,128)S(1)} %add_select_fusion.2) | copy-start | bytes 964
  54.9 12.8 %collective-permute-start.3 = (bf16[96,4096]{1,0:T(8,128)(2,1)}, bf16[96,4096]{1,0:T(8,128)(2,1)S(1)}, u32[]{:S(2)}, u32[]{:S(2)}) collective-permute-start(bf16[96,4096]{1,0:T(8,128)(2,1)} %collective-permute-done.2), channel_id=1, source_target_pairs={{0,1},{1,2},{2,3},{3,4},{4,5},{5,6},{6,7},{7,0},{8,9},{9,10},{10,1... | collective-permute-start | bytes 2359304 | tf_op jit(solution)/shard_map/ppermute | solution.py:62
  55.0 13.1 %collective-permute-start.10 = (bf16[96,4096]{1,0:T(8,128)(2,1)}, bf16[96,4096]{1,0:T(8,128)(2,1)S(1)}, u32[]{:S(2)}, u32[]{:S(2)}) collective-permute-start(bf16[96,4096]{1,0:T(8,128)(2,1)} %collective-permute-done.9), channel_id=1, source_target_pairs={{0,7},{1,0},{2,1},{3,2},{4,3},{5,4},{6,5},{7,6},{8,15},{9,8},{10,9... | collective-permute-start | bytes 2359304 | tf_op jit(solution)/shard_map/ppermute | solution.py:63
  67.8 12.6 %collective-permute-start.4 = (bf16[96,4096]{1,0:T(8,128)(2,1)S(1)}, bf16[96,4096]{1,0:T(8,128)(2,1)S(1)}, u32[]{:S(2)}, u32[]{:S(2)}) collective-permute-start(bf16[96,4096]{1,0:T(8,128)(2,1)S(1)} %collective-permute-done.3), channel_id=1, source_target_pairs={{0,1},{1,2},{2,3},{3,4},{4,5},{5,6},{6,7},{7,0},{8,9},{9,10},{10,1... | collective-permute-start | bytes 2359304 | tf_op jit(solution)/shard_map/ppermute | solution.py:62
  68.0 12.7 %collective-permute-start.11 = (bf16[96,4096]{1,0:T(8,128)(2,1)S(1)}, bf16[96,4096]{1,0:T(8,128)(2,1)S(1)}, u32[]{:S(2)}, u32[]{:S(2)}) collective-permute-start(bf16[96,4096]{1,0:T(8,128)(2,1)S(1)} %collective-permute-done.10), channel_id=1, source_target_pairs={{0,7},{1,0},{2,1},{3,2},{4,3},{5,4},{6,5},{7,6},{8,15},{9,8},{10,9... | collective-permute-start | bytes 2359304 | tf_op jit(solution)/shard_map/ppermute | solution.py:63
  80.4 12.6 %collective-permute-start.5 = (bf16[96,4096]{1,0:T(8,128)(2,1)S(1)}, bf16[96,4096]{1,0:T(8,128)(2,1)S(1)}, u32[]{:S(2)}, u32[]{:S(2)}) collective-permute-start(bf16[96,4096]{1,0:T(8,128)(2,1)S(1)} %collective-permute-done.4), channel_id=1, source_target_pairs={{0,1},{1,2},{2,3},{3,4},{4,5},{5,6},{6,7},{7,0},{8,9},{9,10},{10,1... | collective-permute-start | bytes 2359304 | tf_op jit(solution)/shard_map/ppermute | solution.py:62
  80.8 12.6 %collective-permute-start.12 = (bf16[96,4096]{1,0:T(8,128)(2,1)S(1)}, bf16[96,4096]{1,0:T(8,128)(2,1)S(1)}, u32[]{:S(2)}, u32[]{:S(2)}) collective-permute-start(bf16[96,4096]{1,0:T(8,128)(2,1)S(1)} %collective-permute-done.11), channel_id=1, source_target_pairs={{0,7},{1,0},{2,1},{3,2},{4,3},{5,4},{6,5},{7,6},{8,15},{9,8},{10,9... | collective-permute-start | bytes 2359304 | tf_op jit(solution)/shard_map/ppermute | solution.py:63
  93.0 12.6 %collective-permute-start.6 = (bf16[96,4096]{1,0:T(8,128)(2,1)S(1)}, bf16[96,4096]{1,0:T(8,128)(2,1)S(1)}, u32[]{:S(2)}, u32[]{:S(2)}) collective-permute-start(bf16[96,4096]{1,0:T(8,128)(2,1)S(1)} %collective-permute-done.5), channel_id=1, source_target_pairs={{0,1},{1,2},{2,3},{3,4},{4,5},{5,6},{6,7},{7,0},{8,9},{9,10},{10,1... | collective-permute-start | bytes 2359304 | tf_op jit(solution)/shard_map/ppermute | solution.py:62
  93.4 12.6 %collective-permute-start.13 = (bf16[96,4096]{1,0:T(8,128)(2,1)S(1)}, bf16[96,4096]{1,0:T(8,128)(2,1)S(1)}, u32[]{:S(2)}, u32[]{:S(2)}) collective-permute-start(bf16[96,4096]{1,0:T(8,128)(2,1)S(1)} %collective-permute-done.12), channel_id=1, source_target_pairs={{0,7},{1,0},{2,1},{3,2},{4,3},{5,4},{6,5},{7,6},{8,15},{9,8},{10,9... | collective-permute-start | bytes 2359304 | tf_op jit(solution)/shard_map/ppermute | solution.py:63
  97.8 8.7 %copy-start.7 = (bf16[8,96,8,512]{3,1,2,0:T(8,128)(2,1)}, bf16[8,96,8,512]{3,1,2,0:T(8,128)(2,1)S(1)}, u32[]{:S(2)}) copy-start(bf16[8,96,8,512]{3,1,2,0:T(8,128)(2,1)S(1)} %copy_dynamic-update-slice_fusion.1) | copy-start | bytes 18874372
  106.6 2.6 copy-start.8
  121.5 6.0 %copy-start.19 = (bf16[10]{0:T(256)(128)(2,1)S(1)}, bf16[10]{0:T(256)(128)(2,1)}, u32[]{:S(2)}) copy-start(bf16[10]{0:T(256)(128)(2,1)} %get-tuple-element.45) | copy-start | bytes 64
  125.9 1.6 copy-start.9
  125.9 2.1 copy-start.10
  126.3 1.3 copy-start.1
  132.1 0.7 copy-start.23
  132.1 2.8 copy-start.24
  149.2 4.6 %copy-start.27 = (s32[8,2]{0,1:T(2,128)S(1)}, s32[8,2]{0,1:T(2,128)}, u32[]{:S(2)}) copy-start(s32[8,2]{0,1:T(2,128)} %get-tuple-element.35) | copy-start | bytes 196
  149.2 4.8 %copy-start.29 = (pred[8,2]{0,1:T(4,128)(4,1)S(1)}, pred[8,2]{0,1:T(4,128)(4,1)}, u32[]{:S(2)}) copy-start(pred[8,2]{0,1:T(4,128)(4,1)} %get-tuple-element.33) | copy-start | bytes 52
  149.2 43.1 %all-to-all-start = ((bf16[8,384,512]{2,1,0:T(8,128)(2,1)}), bf16[8,384,512]{2,1,0:T(8,128)(2,1)}, u32[]{:S(2)}, u32[]{:S(2)}) async-start(bf16[8,384,512]{2,1,0:T(8,128)(2,1)} %bitcast.135), calls=%async_computation | async-start | bytes 6291456 | tf_op jit(solution)/shard_map/all_to_all | solution.py:126
  192.3 4.8 %copy-start.16 = (s32[8,10]{1,0:T(8,128)S(1)}, s32[8,10]{1,0:T(8,128)}, u32[]{:S(2)}) copy-start(s32[8,10]{1,0:T(8,128)} %copy-done.15) | copy-start | bytes 964
  192.3 4.8 %copy-start.25 = (pred[8,10]{1,0:T(8,128)(4,1)S(1)}, pred[8,10]{1,0:T(8,128)(4,1)}, u32[]{:S(2)}) copy-start(pred[8,10]{1,0:T(8,128)(4,1)} %get-tuple-element.47) | copy-start | bytes 244
  192.3 4.8 %copy-start.26 = (pred[8,10]{1,0:T(8,128)(4,1)S(1)}, pred[8,10]{1,0:T(8,128)(4,1)}, u32[]{:S(2)}) copy-start(pred[8,10]{1,0:T(8,128)(4,1)} %get-tuple-element.56) | copy-start | bytes 244
  192.3 5.2 %copy-start.14 = (s32[8,10]{1,0:T(8,128)S(1)}, s32[8,10]{1,0:T(8,128)}, u32[]{:S(2)}) copy-start(s32[8,10]{1,0:T(8,128)} %copy-done.13) | copy-start | bytes 964
  192.3 43.0 %all-to-all-start.1 = ((bf16[8,384,512]{2,1,0:T(8,128)(2,1)}), bf16[8,384,512]{2,1,0:T(8,128)(2,1)}, u32[]{:S(2)}, u32[]{:S(2)}) async-start(bf16[8,384,512]{2,1,0:T(8,128)(2,1)} %bitcast.134), calls=%async_computation.1 | async-start | bytes 6291456 | tf_op jit(solution)/shard_map/all_to_all | solution.py:148
  196.9 149.0 %reduce-scatter.7.cloned.1.call-start = ((), (), s32[]{:S(2)}) async-start(), calls=%async_computation.6 | async-start | bytes 8912896
  235.3 4.6 %copy-start.5 = (bf16[192,2048]{1,0:T(8,128)(2,1)S(1)}, bf16[192,2048]{1,0:T(8,128)(2,1)}, u32[]{:S(2)}) copy-start(bf16[192,2048]{1,0:T(8,128)(2,1)} %param.16) | copy-start | bytes 2359300
  235.3 4.6 %copy-start.6 = (f32[192,2048]{1,0:T(8,128)S(1)}, f32[192,2048]{1,0:T(8,128)}, u32[]{:S(2)}) copy-start(f32[192,2048]{1,0:T(8,128)} %get-tuple-element.59) | copy-start | bytes 4718596
  235.3 4.6 %copy-start.21 = (f32[2048]{0:T(1024)S(1)}, f32[2048]{0:T(1024)}, u32[]{:S(2)}) copy-start(f32[2048]{0:T(1024)} %param.15) | copy-start | bytes 24580
  259.8 0.7 copy-start.20
Sparse Core Ops, SparseCore 0:
  10.2 58.9 all-gather.1
  132.3 81.9 reduce-scatter.4
  259.9 85.9 reduce-scatter.6
where the time goes:
time: 356 us; the launch traced here: 355 us
  waiting for transfers between devices  115 us (32%)
  blocking collectives  76.5 us (21%)
  local copies, waits for them, and re-layouts  64.5 us (18%)
  matrix products  34.6 us (10%)
  starting transfers between devices  30.9 us (9%)
  other arithmetic  18.7 us (5%)
  between operations  14.3 us (4%)
    psum x1, blocking collectives, on_device(): lax.psum((jnp.sum(grad_pre, axis=0), jnp.sum(grad_mixed, axis=0)), 'dp')  76.5 us
    ppermute x7, waiting for transfers between devices, ring_gather(): cur_a = lax.ppermute(cur_a, axis, right)  49 us
    unnamed x96, local copies, waits for them, and re-layouts  38.9 us
    all_to_all x1, waiting for transfers between devices, on_device(): lax.all_to_all(pack_parts(back_parts, chosen_in, filled_in), 'tensor', sp...  33.1 us
    all_to_all x1, waiting for transfers between devices, on_device(): lax.all_to_all(pack_parts(parts, chosen_out, filled_out), 'tensor', split...  24.5 us
    ppermute x7, starting transfers between devices, ring_gather(): cur_b = lax.ppermute(cur_b, axis, left)  21.6 us
    mul x2, other arithmetic, pack_parts(): jnp.take(parts, chosen.reshape(-1), axis=0)  7.95 us
    gather x2, local copies, waits for them, and re-layouts, take_blocks(): top = blocks_a[step_a, :, local, :]  7.85 us
  transfers between devices with their start and end apart: 19, of which 14 were waited for; matrix products, arithmetic and copies ran while one was open for 31% of the time, Pallas kernels for 0%

commit v1 on v0

--- a/solution.py
+++ b/solution.py
@@ -5,6 +5,17 @@
 
 BLK = 512
 SLOTS = 10
+
+
+def cut_along(x, dim, count):
+    before, after = (x.shape[:dim], x.shape[dim + 1 :])
+    return jnp.moveaxis(x.reshape(*before, count, -1, *after), dim, 0)
+
+
+def joined_along(blocks, dim):
+    blocks = jnp.moveaxis(blocks, 0, dim)
+    shape = blocks.shape
+    return blocks.reshape(*shape[:dim], shape[dim] * shape[dim + 1], *shape[dim + 2 :])
 
 
 def slot_ranks(owner, alive):
@@ -145,13 +156,15 @@
     )
     back_parts = backward.astype(jnp.bfloat16)
     chosen_in, filled_in = post_table(in_owner[mine], in_rank[mine], alive_mine, groups, capacity)
-    arrived_back = lax.all_to_all(
-        pack_parts(back_parts, chosen_in, filled_in),
-        "tensor",
-        split_axis=0,
-        concat_axis=0,
-        tiled=True,
-    )
+    value = pack_parts(back_parts, chosen_in, filled_in)
+    devices, index = (lax.axis_size("tensor"), lax.axis_index("tensor"))
+    blocks = cut_along(value, 0, devices)
+    outs = [blocks[index]]
+    for step in range(1, devices):
+        sent = blocks[index ^ step]
+        outs.append(lax.ppermute(sent, "tensor", [(i_2, i_2 ^ step) for i_2 in range(devices)]))
+    blocks = jnp.stack(outs)[index ^ jnp.arange(devices)]
+    arrived_back = joined_along(blocks, 0)
     grad_start = collect_parts(
         arrived_back, in_owner, in_local, in_rank, alive, mine, capacity, per_device
     )

time: 356 us -> 359 us (level)
  local copies, waits for them, and re-layouts: 64.5 us -> 70.6 us
  starting transfers between devices: 30.9 us -> 36.3 us
  waiting for transfers between devices: 115 us -> 111 us
  other arithmetic: 18.7 us -> 14.8 us
    ppermute x0 -> x7, waiting for transfers between devices: none -> 48.3 us  [on_device(): lax.ppermute(sent, 'tensor', [(i_2, i_2 ^ step) for i_2 in range(devices)])]
    all_to_all x1 -> x0, waiting for transfers between devices: 33.1 us -> none  [on_device(): lax.all_to_all(pack_parts(back_parts, chosen_in, filled_in), 'tensor', sp...]
    all_to_all x1, waiting for transfers between devices: 24.5 us -> 0.01 us  [on_device(): lax.all_to_all(pack_parts(parts, chosen_out, filled_out), 'tensor', split...]
    ppermute x0 -> x7, starting transfers between devices: none -> 9.57 us  [on_device(): lax.ppermute(sent, 'tensor', [(i_2, i_2 ^ step) for i_2 in range(devices)])]
    all_to_all x1 -> x0, starting transfers between devices: 4.57 us -> none  [on_device(): lax.all_to_all(pack_parts(back_parts, chosen_in, filled_in), 'tensor', sp...]
    gather x0 -> x1, local copies, waits for them, and re-layouts: none -> 4.35 us  [on_device(): blocks = jnp.stack(outs)[index ^ jnp.arange(devices)]]
  transfers between devices with their start and end apart: 19 -> 25, of which waited for: 14 -> 17; matrix products, arithmetic and copies ran while one was open for 31% -> 31% of each run, Pallas kernels for 0% -> 0%
where the time goes in v1:
time: 359 us; the launch traced here: 358 us
  waiting for transfers between devices  111 us (31%)
  blocking collectives  76.5 us (21%)
  local copies, waits for them, and re-layouts  70.6 us (20%)
  starting transfers between devices  36.3 us (10%)
  matrix products  34.4 us (10%)
  other arithmetic  14.8 us (4%)
  between operations  14.4 us (4%)
    psum x1, blocking collectives, on_device(): lax.psum((jnp.sum(grad_pre, axis=0), jnp.sum(grad_mixed, axis=0)), 'dp')  76.5 us
    ppermute x7, waiting for transfers between devices, ring_gather(): cur_a = lax.ppermute(cur_a, axis, right)  52.2 us
    ppermute x7, waiting for transfers between devices, on_device(): lax.ppermute(sent, 'tensor', [(i_2, i_2 ^ step) for i_2 in range(devices)])  48.3 us
    unnamed x96, local copies, waits for them, and re-layouts  39.3 us
    ppermute x7, starting transfers between devices, ring_gather(): cur_b = lax.ppermute(cur_b, axis, left)  22 us
    ppermute x7, starting transfers between devices, on_device(): lax.ppermute(sent, 'tensor', [(i_2, i_2 ^ step) for i_2 in range(devices)])  9.57 us
    unnamed x4, waiting for transfers between devices  8.39 us
    dot_general x2, matrix products, collect_parts(): jnp.einsum('irb,il->rlb', flattened, onehot, preferred_element_type=jnp.f...  7.79 us
  transfers between devices with their start and end apart: 25, of which 17 were waited for; matrix products, arithmetic and copies ran while one was open for 31% of the time, Pallas kernels for 0%

profile of v1, /device:TPU:0, one launch (start us, length us, event | category | flops | bytes accessed | tf_op | source)
XLA Modules:
  0.0 357.8 jit_solution(3610568920145188674)
XLA Ops:
  7.2 0.7 all-gather.2.cloned.1.call-update
  8.3 7.6 %fusion.8 = (f32[2048]{0:T(1024)}, bf16[192,2048]{1,0:T(8,128)(2,1)S(1)}, f32[192,2048]{1,0:T(8,128)}) fusion(bf16[192,2048]{1,0:T(8,128)(2,1)} %param.16, f32[2048]{0:T(1024)} %param.13, bf16[192,2048]{1,0:T(8,128)(2,1)S(1)} %copy-done, bf16[2048,2048]{1,0:T(8,128)(2,1)} %param.12), kind=kOutput, calls=%fused_computation.31 | convolution fusion | flops 1614542848 | bytes 12337152 | tf_op jit(solution)/shard_map/dot_general | solution.py:108
  16.3 2.9 collective-permute-start.7
  19.3 9.8 %collective-permute-done = bf16[96,4096]{1,0:T(8,128)(2,1)} collective-permute-done((bf16[96,4096]{1,0:T(8,128)(2,1)S(1)}, bf16[96,4096]{1,0:T(8,128)(2,1)}, u32[]{:S(2)}, u32[]{:S(2)}) %collective-permute-start) | collective-permute-done | bytes 786464 | tf_op jit(solution)/shard_map/ppermute | solution.py:73
  29.1 3.0 collective-permute-start.8
  32.7 9.3 %collective-permute-done.1 = bf16[96,4096]{1,0:T(8,128)(2,1)} collective-permute-done((bf16[96,4096]{1,0:T(8,128)(2,1)}, bf16[96,4096]{1,0:T(8,128)(2,1)}, u32[]{:S(2)}, u32[]{:S(2)}) %collective-permute-start.1) | collective-permute-done | bytes 786464 | tf_op jit(solution)/shard_map/ppermute | solution.py:73
  42.0 3.0 collective-permute-start.9
  46.7 1.4 copy.128
  48.1 1.4 copy.136
  49.5 5.3 %collective-permute-done.2 = bf16[96,4096]{1,0:T(8,128)(2,1)S(1)} collective-permute-done((bf16[96,4096]{1,0:T(8,128)(2,1)}, bf16[96,4096]{1,0:T(8,128)(2,1)S(1)}, u32[]{:S(2)}, u32[]{:S(2)}) %collective-permute-start.2) | collective-permute-done | bytes 786464 | tf_op jit(solution)/shard_map/ppermute | solution.py:73
  54.8 3.4 collective-permute-start.10
  58.7 1.4 copy.129
  60.1 1.4 copy.137
  61.7 5.7 %collective-permute-done.3 = bf16[96,4096]{1,0:T(8,128)(2,1)S(1)} collective-permute-done((bf16[96,4096]{1,0:T(8,128)(2,1)S(1)}, bf16[96,4096]{1,0:T(8,128)(2,1)S(1)}, u32[]{:S(2)}, u32[]{:S(2)}) %collective-permute-start.3) | collective-permute-done | bytes 786464 | tf_op jit(solution)/shard_map/ppermute | solution.py:73
  67.7 3.5 collective-permute-start.11
  73.1 7.0 %collective-permute-done.4 = bf16[96,4096]{1,0:T(8,128)(2,1)S(1)} collective-permute-done((bf16[96,4096]{1,0:T(8,128)(2,1)S(1)}, bf16[96,4096]{1,0:T(8,128)(2,1)S(1)}, u32[]{:S(2)}, u32[]{:S(2)}) %collective-permute-start.4) | collective-permute-done | bytes 786464 | tf_op jit(solution)/shard_map/ppermute | solution.py:73
  80.7 3.1 collective-permute-start.12
  85.1 7.6 %collective-permute-done.5 = bf16[96,4096]{1,0:T(8,128)(2,1)S(1)} collective-permute-done((bf16[96,4096]{1,0:T(8,128)(2,1)S(1)}, bf16[96,4096]{1,0:T(8,128)(2,1)S(1)}, u32[]{:S(2)}, u32[]{:S(2)}) %collective-permute-start.5) | collective-permute-done | bytes 786464 | tf_op jit(solution)/shard_map/ppermute | solution.py:73
  93.3 3.1 collective-permute-start.13
  97.8 7.6 %collective-permute-done.6 = bf16[96,4096]{1,0:T(8,128)(2,1)S(1)} collective-permute-done((bf16[96,4096]{1,0:T(8,128)(2,1)S(1)}, bf16[96,4096]{1,0:T(8,128)(2,1)S(1)}, u32[]{:S(2)}, u32[]{:S(2)}) %collective-permute-start.6) | collective-permute-done | bytes 786464 | tf_op jit(solution)/shard_map/ppermute | solution.py:73
  106.5 2.6 copy-done.6
  109.1 3.4 gather_fusion
  112.5 4.4 %gather_fusion.2 = bf16[10,96,512]{2,1,0:T(8,128)(2,1)} fusion(bf16[8,96,8,512]{3,1,2,0:T(8,128)(2,1)} %copy-done.6, s32[10]{0:T(128)S(1)} %get-tuple-element.60), kind=kCustom, calls=%fused_computation.4 | custom fusion | bytes 1966160 | tf_op jit(solution)/shard_map/gather | solution.py:86
  116.9 1.1 copy_dynamic-update-slice_fusion
  118.0 3.4 gather_fusion.1
  121.5 4.4 %gather_fusion.3 = bf16[10,96,512]{2,1,0:T(8,128)(2,1)} fusion(bf16[8,96,8,512]{3,1,2,0:T(8,128)(2,1)} %copy_dynamic-update-slice_fusion, s32[10]{0:T(128)S(1)} %get-tuple-element.61), kind=kCustom, calls=%fused_computation.5 | custom fusion | bytes 1966160 | tf_op jit(solution)/shard_map/gather | solution.py:87
  126.0 1.3 copy-done.1
  127.4 0.7 copy-done.8
  128.1 4.1 %convolution_convert_fusion = bf16[10,512,512]{2,1,0:T(8,128)(2,1)} fusion(bf16[10,192,512]{2,1,0:T(8,128)(2,1)S(1)} %constant_dynamic-update-slice_fusion, bf16[10,96,512]{2,1,0:T(8,128)(2,1)S(1)} %copy-done.8, bf16[10,96,512]{2,1,0:T(8,128)(2,1)S(1)} %copy-done.7, bf16[10]{0:T(256)(128)(2,1)S(1)} %copy-done.15), kind=kOutput, calls=%fused_computation.14 | convolution fusion | flops 1015152640 | bytes 9175060 | tf_op jit(solution)/shard_map/kri,krj->kij/dot_general | solution.py:171
  137.8 4.3 %convert_multiply_fusion.2 = bf16[10,192,512]{2,1,0:T(8,128)(2,1)S(1)} fusion(bf16[10,192,512]{2,1,0:T(8,128)(2,1)} %copy-done.1, bf16[10,512,512]{2,1,0:T(8,128)(2,1)} %all-gather.2.cloned.1.call-done, bf16[10]{0:T(256)(128)(2,1)} %get-tuple-element.45), kind=kOutput, calls=%fused_computation.21 | convolution fusion | flops 1008599040 | bytes 9175060 | tf_op jit(solution)/shard_map/kri,kij->krj/dot_general | solution.py:127
  142.1 2.4 gather_fusion.5
  144.6 4.0 %select_multiply_fusion.1 = bf16[16,192,512]{2,1,0:T(8,128)(2,1)} fusion(bf16[16,192,512]{2,1,0:T(8,128)(2,1)} %gather_fusion.5, pred[16]{0:T(512)(128)(4,1)} %get-tuple-element.73, bf16[16]{0:T(256)(128)(2,1)} %reshape.566), kind=kLoop, calls=%fused_computation.13 | loop fusion | flops 3145728 | bytes 6291504 | tf_op jit(solution)/shard_map/mul | solution.py:41
  148.5 4.6 %all-to-all-start = ((bf16[8,384,512]{2,1,0:T(8,128)(2,1)}), bf16[8,384,512]{2,1,0:T(8,128)(2,1)}, u32[]{:S(2)}, u32[]{:S(2)}) async-start(bf16[8,384,512]{2,1,0:T(8,128)(2,1)} %bitcast.163), calls=%async_computation | async-start | bytes 6291456 | tf_op jit(solution)/shard_map/all_to_all | solution.py:137
  153.2 5.1 %convolution_convert_fusion.1 = bf16[10,192,512]{2,1,0:T(8,128)(2,1)S(1)} fusion(bf16[10,512,512]{2,1,0:T(8,128)(2,1)} %all-gather.2.cloned.1.call-done, bf16[10,96,512]{2,1,0:T(8,128)(2,1)} %gather_fusion.3, bf16[10,96,512]{2,1,0:T(8,128)(2,1)} %gather_fusion.2, bf16[10]{0:T(256)(128)(2,1)S(1)} %copy-done.16), kind=kOutput, calls=%fused_computation.22 | convolution fusion | flops 1013514240 | bytes 9175060 | tf_op jit(solution)/shard_map/krj,kij->kri/dot_general | solution.py:151
  158.3 2.5 gather_fusion.6
  160.8 2.3 select_multiply_fusion
  163.2 1.6 dynamic-slice_bitcast_fusion
  165.7 1.8 collective-permute-start.15
  167.8 3.0 collective-permute-start.17
  171.1 3.1 collective-permute-start.19
  174.2 0.8 bitcast_dynamic-update-slice_fusion.6
  174.9 24.0 %collective-permute-done.15 = bf16[1,384,512]{2,1,0:T(8,128)(2,1)S(1)} collective-permute-done((bf16[1,384,512]{2,1,0:T(8,128)(2,1)}, bf16[1,384,512]{2,1,0:T(8,128)(2,1)S(1)}, u32[]{:S(2)}, u32[]{:S(2)}) %collective-permute-start.15) | collective-permute-done | bytes 393248 | tf_op jit(solution)/shard_map/ppermute | solution.py:165
  198.9 0.8 collective-permute-start.20
  199.7 0.8 bitcast_dynamic-update-slice_fusion.5
  200.5 5.8 %collective-permute-done.16 = bf16[1,384,512]{2,1,0:T(8,128)(2,1)S(1)} collective-permute-done((bf16[1,384,512]{2,1,0:T(8,128)(2,1)}, bf16[1,384,512]{2,1,0:T(8,128)(2,1)S(1)}, u32[]{:S(2)}, u32[]{:S(2)}) %collective-permute-start.16) | collective-permute-done | bytes 393248 | tf_op jit(solution)/shard_map/ppermute | solution.py:165
  206.4 0.8 bitcast_dynamic-update-slice_fusion.4
  207.2 10.2 %collective-permute-done.17 = bf16[1,384,512]{2,1,0:T(8,128)(2,1)S(1)} collective-permute-done((bf16[1,384,512]{2,1,0:T(8,128)(2,1)}, bf16[1,384,512]{2,1,0:T(8,128)(2,1)S(1)}, u32[]{:S(2)}, u32[]{:S(2)}) %collective-permute-start.17) | collective-permute-done | bytes 393248 | tf_op jit(solution)/shard_map/ppermute | solution.py:165
  217.4 0.8 bitcast_dynamic-update-slice_fusion.3
  218.1 6.7 %collective-permute-done.18 = bf16[1,384,512]{2,1,0:T(8,128)(2,1)S(1)} collective-permute-done((bf16[1,384,512]{2,1,0:T(8,128)(2,1)}, bf16[1,384,512]{2,1,0:T(8,128)(2,1)S(1)}, u32[]{:S(2)}, u32[]{:S(2)}) %collective-permute-start.18) | collective-permute-done | bytes 393248 | tf_op jit(solution)/shard_map/ppermute | solution.py:165
  224.8 0.8 bitcast_dynamic-update-slice_fusion.2
  225.6 0.8 bitcast_dynamic-update-slice_fusion.1
  226.4 1.6 collective-permute-done.20
  228.0 0.8 bitcast_dynamic-update-slice_fusion
  228.8 4.3 %gather_fusion.4 = bf16[8,384,512]{2,1,0:T(8,128)(2,1)} fusion(bf16[8,384,512]{2,1,0:T(8,128)(2,1)} %bitcast.170, s32[1024]{0:T(1024)S(1)} %pad_clamp_fusion), kind=kCustom, calls=%fused_computation.6 | custom fusion | bytes 6291488 | tf_op jit(solution)/shard_map/gather | solution.py:166
  233.1 3.8 %fusion = f32[4,192,512]{2,0,1:T(4,128)S(1)} fusion(bf16[16,4,1]{1,0,2:T(8,128)(2,1)S(1)} %bitcast.200, bf16[16,192,512]{2,1,0:T(8,128)(2,1)} %bitcast.164), kind=kOutput, calls=%fused_computation.8 | convolution fusion | flops 12582912 | bytes 4718720 | tf_op jit(solution)/shard_map/irb,il->rlb/dot_general | solution.py:62
  237.6 4.0 %fusion.2 = f32[4,192,512]{2,0,1:T(4,128)S(1)} fusion(bf16[16,4,1]{1,0,2:T(8,128)(2,1)S(1)} %bitcast.199, bf16[16,192,512]{2,1,0:T(8,128)(2,1)} %bitcast.10), kind=kOutput, calls=%fused_computation.10 | convolution fusion | flops 12582912 | bytes 4718720 | tf_op jit(solution)/shard_map/irb,il->rlb/dot_general | solution.py:62
  242.2 1.9 fusion.53
  244.1 5.6 %convert_bitcast_fusion = bf16[2048,2048]{0,1:T(8,128)(2,1)} fusion(bf16[192,2048]{1,0:T(8,128)(2,1)S(1)} %copy-done, bf16[192,2048]{1,0:T(8,128)(2,1)S(1)} %get-tuple-element.42), kind=kOutput, calls=%fused_computation.7 | convolution fusion | flops 1614807040 | bytes 9961472 | tf_op jit(solution)/shard_map/dot_general | solution.py:181
  249.7 12.3 %copy.125 = bf16[2048,2048]{1,0:T(8,128)(2,1)} copy(bf16[2048,2048]{0,1:T(8,128)(2,1)} %convert_bitcast_fusion) | data formatting | bytes 16777216
  262.7 76.5 %all-reduce = (f32[2048]{0:T(1024)}, f32[2048]{0:T(1024)}) all-reduce(f32[2048]{0:T(1024)S(1)} %get-tuple-element.41, f32[2048]{0:T(1024)S(1)} %copy-done.18), channel_id=1, replica_groups=mesh['dp'=16,'tensor'=8] {'dp'}, use_global_device_ids=true, to_apply=%region_10.12 | all-reduce | flops 4096 | bytes 32768 | tf_op jit(solution)/shard_map/psum | solution.py:188
  339.2 1.9 convert_element_type.131
  341.1 7.7 %reduce-scatter.7.cloned.1.call-done = bf16[128,2048]{1,0:T(8,128)(2,1)} async-done(((bf16[2048,2048]{1,0:T(8,128)(2,1)}), bf16[128,2048]{1,0:T(8,128)(2,1)}) %reduce-scatter.7.cloned.1.call-update) | async-done | bytes 524304
  348.8 1.3 copy.126
  350.1 1.2 copy.120
  (157 shorter events, 20.3 us)
Async XLA Ops:
  7.2 1.1 copy-start
  7.2 130.6 %all-gather.2.cloned.1.call-start = ((), (), s32[]{:S(2)}) async-start(), calls=%async_computation.3 | async-start | bytes 5570560 | tf_op jit(solution)/shard_map/all_gather | solution.py:130
  7.9 8.0 %copy-start.2 = (bf16[192,2048]{1,0:T(8,128)(2,1)S(1)}, bf16[192,2048]{1,0:T(8,128)(2,1)}, u32[]{:S(2)}) copy-start(bf16[192,2048]{1,0:T(8,128)(2,1)} %param.16) | copy-start | bytes 2359300
  7.9 331.3 %reduce-scatter.5.cloned.1.call-start = ((), (), s32[]{:S(2)}) async-start(), calls=%async_computation.4 | async-start | bytes 5570560 | tf_op jit(solution)/shard_map/reduce_scatter | solution.py:172
  15.9 16.1 %copy-start.13 = (s32[8,10]{1,0:T(8,128)S(1)}, s32[8,10]{1,0:T(8,128)}, u32[]{:S(2)}) copy-start(s32[8,10]{1,0:T(8,128)} %param.17) | copy-start | bytes 964
  15.9 16.1 %copy-start.14 = (s32[8,10]{1,0:T(8,128)S(1)}, s32[8,10]{1,0:T(8,128)}, u32[]{:S(2)}) copy-start(s32[8,10]{1,0:T(8,128)} %param.18) | copy-start | bytes 964
  15.9 16.2 %copy-start.26 = (s32[8]{0:T(128)S(1)}, s32[8]{0:T(128)}, u32[]{:S(2)}) copy-start(s32[8]{0:T(128)} %param.19) | copy-start | bytes 100
  16.3 12.7 %collective-permute-start = (bf16[96,4096]{1,0:T(8,128)(2,1)S(1)}, bf16[96,4096]{1,0:T(8,128)(2,1)}, u32[]{:S(2)}, u32[]{:S(2)}) collective-permute-start(bf16[96,4096]{1,0:T(8,128)(2,1)S(1)} %get-tuple-element.59), channel_id=1, source_target_pairs={{0,1},{1,2},{2,3},{3,4},{4,5},{5,6},{6,7},{7,0},{8,9},{9,10},{10,1... | collective-permute-start | bytes 2359304 | tf_op jit(solution)/shard_map/ppermute | solution.py:73
  16.3 12.7 %collective-permute-start.7 = (bf16[96,4096]{1,0:T(8,128)(2,1)S(1)}, bf16[96,4096]{1,0:T(8,128)(2,1)}, u32[]{:S(2)}, u32[]{:S(2)}) collective-permute-start(bf16[96,4096]{1,0:T(8,128)(2,1)S(1)} %get-tuple-element.58), channel_id=1, source_target_pairs={{0,7},{1,0},{2,1},{3,2},{4,3},{5,4},{6,5},{7,6},{8,15},{9,8},{10,9... | collective-permute-start | bytes 2359304 | tf_op jit(solution)/shard_map/ppermute | solution.py:74
  29.0 12.9 %collective-permute-start.1 = (bf16[96,4096]{1,0:T(8,128)(2,1)}, bf16[96,4096]{1,0:T(8,128)(2,1)}, u32[]{:S(2)}, u32[]{:S(2)}) collective-permute-start(bf16[96,4096]{1,0:T(8,128)(2,1)} %collective-permute-done), channel_id=1, source_target_pairs={{0,1},{1,2},{2,3},{3,4},{4,5},{5,6},{6,7},{7,0},{8,9},{9,10},{10,1... | collective-permute-start | bytes 2359304 | tf_op jit(solution)/shard_map/ppermute | solution.py:73
  29.1 12.9 %collective-permute-start.8 = (bf16[96,4096]{1,0:T(8,128)(2,1)}, bf16[96,4096]{1,0:T(8,128)(2,1)}, u32[]{:S(2)}, u32[]{:S(2)}) collective-permute-start(bf16[96,4096]{1,0:T(8,128)(2,1)} %collective-permute-done.7), channel_id=1, source_target_pairs={{0,7},{1,0},{2,1},{3,2},{4,3},{5,4},{6,5},{7,6},{8,15},{9,8},{10,9... | collective-permute-start | bytes 2359304 | tf_op jit(solution)/shard_map/ppermute | solution.py:74
  32.0 14.1 %copy-start.9 = (s32[8,10]{1,0:T(8,128)}, s32[8,10]{1,0:T(8,128)S(1)}, u32[]{:S(2)}) copy-start(s32[8,10]{1,0:T(8,128)S(1)} %get-tuple-element.68) | copy-start | bytes 964
  32.0 14.6 %copy-start.11 = (s32[8,10]{1,0:T(8,128)}, s32[8,10]{1,0:T(8,128)S(1)}, u32[]{:S(2)}) copy-start(s32[8,10]{1,0:T(8,128)S(1)} %get-tuple-element.69) | copy-start | bytes 964
  32.7 13.9 %copy-start.20 = (pred[8,10]{1,0:T(8,128)(4,1)}, pred[8,10]{1,0:T(8,128)(4,1)S(1)}, u32[]{:S(2)}) copy-start(pred[8,10]{1,0:T(8,128)(4,1)S(1)} %get-tuple-element.66) | copy-start | bytes 244
  42.0 12.8 %collective-permute-start.2 = (bf16[96,4096]{1,0:T(8,128)(2,1)}, bf16[96,4096]{1,0:T(8,128)(2,1)S(1)}, u32[]{:S(2)}, u32[]{:S(2)}) collective-permute-start(bf16[96,4096]{1,0:T(8,128)(2,1)} %collective-permute-done.1), channel_id=1, source_target_pairs={{0,1},{1,2},{2,3},{3,4},{4,5},{5,6},{6,7},{7,0},{8,9},{9,10},{10,1... | collective-permute-start | bytes 2359304 | tf_op jit(solution)/shard_map/ppermute | solution.py:73
  42.0 12.8 %collective-permute-start.9 = (bf16[96,4096]{1,0:T(8,128)(2,1)}, bf16[96,4096]{1,0:T(8,128)(2,1)S(1)}, u32[]{:S(2)}, u32[]{:S(2)}) collective-permute-start(bf16[96,4096]{1,0:T(8,128)(2,1)} %collective-permute-done.8), channel_id=1, source_target_pairs={{0,7},{1,0},{2,1},{3,2},{4,3},{5,4},{6,5},{7,6},{8,15},{9,8},{10,9... | collective-permute-start | bytes 2359304 | tf_op jit(solution)/shard_map/ppermute | solution.py:74
  54.8 12.6 %collective-permute-start.3 = (bf16[96,4096]{1,0:T(8,128)(2,1)S(1)}, bf16[96,4096]{1,0:T(8,128)(2,1)S(1)}, u32[]{:S(2)}, u32[]{:S(2)}) collective-permute-start(bf16[96,4096]{1,0:T(8,128)(2,1)S(1)} %collective-permute-done.2), channel_id=1, source_target_pairs={{0,1},{1,2},{2,3},{3,4},{4,5},{5,6},{6,7},{7,0},{8,9},{9,10},{10,1... | collective-permute-start | bytes 2359304 | tf_op jit(solution)/shard_map/ppermute | solution.py:73
  54.8 12.9 %collective-permute-start.10 = (bf16[96,4096]{1,0:T(8,128)(2,1)S(1)}, bf16[96,4096]{1,0:T(8,128)(2,1)S(1)}, u32[]{:S(2)}, u32[]{:S(2)}) collective-permute-start(bf16[96,4096]{1,0:T(8,128)(2,1)S(1)} %collective-permute-done.9), channel_id=1, source_target_pairs={{0,7},{1,0},{2,1},{3,2},{4,3},{5,4},{6,5},{7,6},{8,15},{9,8},{10,9... | collective-permute-start | bytes 2359304 | tf_op jit(solution)/shard_map/ppermute | solution.py:74
  67.5 12.6 %collective-permute-start.4 = (bf16[96,4096]{1,0:T(8,128)(2,1)S(1)}, bf16[96,4096]{1,0:T(8,128)(2,1)S(1)}, u32[]{:S(2)}, u32[]{:S(2)}) collective-permute-start(bf16[96,4096]{1,0:T(8,128)(2,1)S(1)} %collective-permute-done.3), channel_id=1, source_target_pairs={{0,1},{1,2},{2,3},{3,4},{4,5},{5,6},{6,7},{7,0},{8,9},{9,10},{10,1... | collective-permute-start | bytes 2359304 | tf_op jit(solution)/shard_map/ppermute | solution.py:73
  67.7 13.0 %collective-permute-start.11 = (bf16[96,4096]{1,0:T(8,128)(2,1)S(1)}, bf16[96,4096]{1,0:T(8,128)(2,1)S(1)}, u32[]{:S(2)}, u32[]{:S(2)}) collective-permute-start(bf16[96,4096]{1,0:T(8,128)(2,1)S(1)} %collective-permute-done.10), channel_id=1, source_target_pairs={{0,7},{1,0},{2,1},{3,2},{4,3},{5,4},{6,5},{7,6},{8,15},{9,8},{10,9... | collective-permute-start | bytes 2359304 | tf_op jit(solution)/shard_map/ppermute | solution.py:74
  80.1 12.6 %collective-permute-start.5 = (bf16[96,4096]{1,0:T(8,128)(2,1)S(1)}, bf16[96,4096]{1,0:T(8,128)(2,1)S(1)}, u32[]{:S(2)}, u32[]{:S(2)}) collective-permute-start(bf16[96,4096]{1,0:T(8,128)(2,1)S(1)} %collective-permute-done.4), channel_id=1, source_target_pairs={{0,1},{1,2},{2,3},{3,4},{4,5},{5,6},{6,7},{7,0},{8,9},{9,10},{10,1... | collective-permute-start | bytes 2359304 | tf_op jit(solution)/shard_map/ppermute | solution.py:73
  80.7 12.6 %collective-permute-start.12 = (bf16[96,4096]{1,0:T(8,128)(2,1)S(1)}, bf16[96,4096]{1,0:T(8,128)(2,1)S(1)}, u32[]{:S(2)}, u32[]{:S(2)}) collective-permute-start(bf16[96,4096]{1,0:T(8,128)(2,1)S(1)} %collective-permute-done.11), channel_id=1, source_target_pairs={{0,7},{1,0},{2,1},{3,2},{4,3},{5,4},{6,5},{7,6},{8,15},{9,8},{10,9... | collective-permute-start | bytes 2359304 | tf_op jit(solution)/shard_map/ppermute | solution.py:74
  92.7 12.6 %collective-permute-start.6 = (bf16[96,4096]{1,0:T(8,128)(2,1)S(1)}, bf16[96,4096]{1,0:T(8,128)(2,1)S(1)}, u32[]{:S(2)}, u32[]{:S(2)}) collective-permute-start(bf16[96,4096]{1,0:T(8,128)(2,1)S(1)} %collective-permute-done.5), channel_id=1, source_target_pairs={{0,1},{1,2},{2,3},{3,4},{4,5},{5,6},{6,7},{7,0},{8,9},{9,10},{10,1... | collective-permute-start | bytes 2359304 | tf_op jit(solution)/shard_map/ppermute | solution.py:73
  93.3 12.6 %collective-permute-start.13 = (bf16[96,4096]{1,0:T(8,128)(2,1)S(1)}, bf16[96,4096]{1,0:T(8,128)(2,1)S(1)}, u32[]{:S(2)}, u32[]{:S(2)}) collective-permute-start(bf16[96,4096]{1,0:T(8,128)(2,1)S(1)} %collective-permute-done.12), channel_id=1, source_target_pairs={{0,7},{1,0},{2,1},{3,2},{4,3},{5,4},{6,5},{7,6},{8,15},{9,8},{10,9... | collective-permute-start | bytes 2359304 | tf_op jit(solution)/shard_map/ppermute | solution.py:74
  97.7 8.7 %copy-start.5 = (bf16[8,96,8,512]{3,1,2,0:T(8,128)(2,1)}, bf16[8,96,8,512]{3,1,2,0:T(8,128)(2,1)S(1)}, u32[]{:S(2)}) copy-start(bf16[8,96,8,512]{3,1,2,0:T(8,128)(2,1)S(1)} %copy_dynamic-update-slice_fusion.1) | copy-start | bytes 18874372
  106.5 2.6 copy-start.6
  121.5 5.8 %copy-start.15 = (bf16[10]{0:T(256)(128)(2,1)S(1)}, bf16[10]{0:T(256)(128)(2,1)}, u32[]{:S(2)}) copy-start(bf16[10]{0:T(256)(128)(2,1)} %get-tuple-element.45) | copy-start | bytes 64
  125.8 1.5 copy-start.7
  125.8 2.2 copy-start.8
  126.0 1.3 copy-start.1
  132.1 0.7 copy-start.21
  132.1 1.8 copy-start.22
  132.1 5.0 %copy-start.12 = (s32[8,10]{1,0:T(8,128)S(1)}, s32[8,10]{1,0:T(8,128)}, u32[]{:S(2)}) copy-start(s32[8,10]{1,0:T(8,128)} %copy-done.11) | copy-start | bytes 964
  132.1 5.1 %copy-start.10 = (s32[8,10]{1,0:T(8,128)S(1)}, s32[8,10]{1,0:T(8,128)}, u32[]{:S(2)}) copy-start(s32[8,10]{1,0:T(8,128)} %copy-done.9) | copy-start | bytes 964
  132.1 5.1 %copy-start.23 = (pred[8,10]{1,0:T(8,128)(4,1)S(1)}, pred[8,10]{1,0:T(8,128)(4,1)}, u32[]{:S(2)}) copy-start(pred[8,10]{1,0:T(8,128)(4,1)} %get-tuple-element.47) | copy-start | bytes 244
  132.1 5.1 %copy-start.24 = (pred[8,10]{1,0:T(8,128)(4,1)S(1)}, pred[8,10]{1,0:T(8,128)(4,1)}, u32[]{:S(2)}) copy-start(pred[8,10]{1,0:T(8,128)(4,1)} %get-tuple-element.64) | copy-start | bytes 244
  148.5 4.7 %copy-start.16 = (bf16[10]{0:T(256)(128)(2,1)S(1)}, bf16[10]{0:T(256)(128)(2,1)}, u32[]{:S(2)}) copy-start(bf16[10]{0:T(256)(128)(2,1)} %get-tuple-element.45) | copy-start | bytes 64
  148.5 89.0 %all-to-all-start = ((bf16[8,384,512]{2,1,0:T(8,128)(2,1)}), bf16[8,384,512]{2,1,0:T(8,128)(2,1)}, u32[]{:S(2)}, u32[]{:S(2)}) async-start(bf16[8,384,512]{2,1,0:T(8,128)(2,1)} %bitcast.163), calls=%async_computation | async-start | bytes 6291456 | tf_op jit(solution)/shard_map/all_to_all | solution.py:137
  153.1 195.7 %reduce-scatter.7.cloned.1.call-start = ((), (), s32[]{:S(2)}) async-start(), calls=%async_computation.5 | async-start | bytes 8912896
  158.3 2.6 copy-start.25
  163.1 2.1 copy-start.17
  164.7 6.3 %collective-permute-start.14 = (bf16[1,384,512]{2,1,0:T(8,128)(2,1)S(1)}, bf16[1,384,512]{2,1,0:T(8,128)(2,1)S(1)}, u32[]{:S(2)}, u32[]{:S(2)}) collective-permute-start(bf16[1,384,512]{2,1,0:T(8,128)(2,1)S(1)} %get-tuple-element.55), channel_id=1, source_target_pairs={{0,1},{1,0},{2,3},{3,2},{4,5},{5,4},{6,7},{7,6},{8,9},{9,8},{10,11... | collective-permute-start | bytes 1179656 | tf_op jit(solution)/shard_map/ppermute | solution.py:165
  165.7 33.2 %collective-permute-start.15 = (bf16[1,384,512]{2,1,0:T(8,128)(2,1)}, bf16[1,384,512]{2,1,0:T(8,128)(2,1)S(1)}, u32[]{:S(2)}, u32[]{:S(2)}) collective-permute-start(bf16[1,384,512]{2,1,0:T(8,128)(2,1)} %get-tuple-element.54), channel_id=1, source_target_pairs={{0,2},{1,3},{2,0},{3,1},{4,6},{5,7},{6,4},{7,5},{8,10},{9,11},{10,... | collective-permute-start | bytes 1179656 | tf_op jit(solution)/shard_map/ppermute | solution.py:165
  167.7 38.7 %collective-permute-start.16 = (bf16[1,384,512]{2,1,0:T(8,128)(2,1)}, bf16[1,384,512]{2,1,0:T(8,128)(2,1)S(1)}, u32[]{:S(2)}, u32[]{:S(2)}) collective-permute-start(bf16[1,384,512]{2,1,0:T(8,128)(2,1)} %get-tuple-element.53), channel_id=1, source_target_pairs={{0,3},{1,2},{2,1},{3,0},{4,7},{5,6},{6,5},{7,4},{8,11},{9,10},{10,... | collective-permute-start | bytes 1179656 | tf_op jit(solution)/shard_map/ppermute | solution.py:165
  167.8 49.6 %collective-permute-start.17 = (bf16[1,384,512]{2,1,0:T(8,128)(2,1)}, bf16[1,384,512]{2,1,0:T(8,128)(2,1)S(1)}, u32[]{:S(2)}, u32[]{:S(2)}) collective-permute-start(bf16[1,384,512]{2,1,0:T(8,128)(2,1)} %get-tuple-element.52), channel_id=1, source_target_pairs={{0,4},{1,5},{2,6},{3,7},{4,0},{5,1},{6,2},{7,3},{8,12},{9,13},{10,... | collective-permute-start | bytes 1179656 | tf_op jit(solution)/shard_map/ppermute | solution.py:165
  170.8 54.1 %collective-permute-start.18 = (bf16[1,384,512]{2,1,0:T(8,128)(2,1)}, bf16[1,384,512]{2,1,0:T(8,128)(2,1)S(1)}, u32[]{:S(2)}, u32[]{:S(2)}) collective-permute-start(bf16[1,384,512]{2,1,0:T(8,128)(2,1)} %get-tuple-element.51), channel_id=1, source_target_pairs={{0,5},{1,4},{2,7},{3,6},{4,1},{5,0},{6,3},{7,2},{8,13},{9,12},{10,... | collective-permute-start | bytes 1179656 | tf_op jit(solution)/shard_map/ppermute | solution.py:165
  171.1 54.5 %collective-permute-start.19 = (bf16[1,384,512]{2,1,0:T(8,128)(2,1)}, bf16[1,384,512]{2,1,0:T(8,128)(2,1)S(1)}, u32[]{:S(2)}, u32[]{:S(2)}) collective-permute-start(bf16[1,384,512]{2,1,0:T(8,128)(2,1)} %get-tuple-element.50), channel_id=1, source_target_pairs={{0,6},{1,7},{2,4},{3,5},{4,2},{5,3},{6,0},{7,1},{8,14},{9,15},{10,... | collective-permute-start | bytes 1179656 | tf_op jit(solution)/shard_map/ppermute | solution.py:165
  198.9 29.1 %collective-permute-start.20 = (bf16[1,384,512]{2,1,0:T(8,128)(2,1)}, bf16[1,384,512]{2,1,0:T(8,128)(2,1)S(1)}, u32[]{:S(2)}, u32[]{:S(2)}) collective-permute-start(bf16[1,384,512]{2,1,0:T(8,128)(2,1)} %get-tuple-element.49), channel_id=1, source_target_pairs={{0,7},{1,6},{2,5},{3,4},{4,3},{5,2},{6,1},{7,0},{8,15},{9,14},{10,... | collective-permute-start | bytes 1179656 | tf_op jit(solution)/shard_map/ppermute | solution.py:165
  237.6 4.6 %copy-start.3 = (bf16[192,2048]{1,0:T(8,128)(2,1)S(1)}, bf16[192,2048]{1,0:T(8,128)(2,1)}, u32[]{:S(2)}) copy-start(bf16[192,2048]{1,0:T(8,128)(2,1)} %param.16) | copy-start | bytes 2359300
  237.6 4.6 %copy-start.4 = (f32[192,2048]{1,0:T(8,128)S(1)}, f32[192,2048]{1,0:T(8,128)}, u32[]{:S(2)}) copy-start(f32[192,2048]{1,0:T(8,128)} %get-tuple-element.67) | copy-start | bytes 4718596
  237.6 4.6 %copy-start.19 = (f32[2048]{0:T(1024)S(1)}, f32[2048]{0:T(1024)}, u32[]{:S(2)}) copy-start(f32[2048]{0:T(1024)} %param.15) | copy-start | bytes 24580
  262.0 0.7 copy-start.18
Sparse Core Ops, SparseCore 0:
  10.2 58.9 all-gather.1
  132.3 81.8 reduce-scatter.4
  262.2 86.6 reduce-scatter.6
